TPU v7x, 32 devices: a whole 2x2x4 slice. The times are simulated.
32 devices in a mesh: pipe: 2 (over core), ctx: 8 (over z, x), tp: 2 (over y).
Axes of the slice: x: 2, y: 2, z: 4, core: 2. Of those that a mesh axis runs over, the one named last changes fastest.
Arguments:
- tokens: bfloat16 [1, 1024, 4096], P(None, ('ctx', 'tp')), may hold values from -6 to 6
- norm_gain: bfloat16 [2, 4096], P('pipe'), may hold values from 0.099609375 to 1.8984375
- query_weight: bfloat16 [2, 4096, 4096], P('pipe', 'ctx', 'tp'), may hold values from -0.1875 to 0.1875
- keyval_weight: bfloat16 [2, 4096, 2048], P('pipe', None, 'tp'), may hold values from -0.1875 to 0.1875
- output_weight: bfloat16 [2, 4096, 4096], P('pipe', 'tp', 'ctx'), may hold values from -0.09375 to 0.09375
Outputs:
- states: bfloat16 [2, 1, 1024, 4096], P('pipe', None, ('ctx', 'tp'))
All inputs are finite; a program needn't handle non-finite values.
Results may differ from a plain program's by a relative error of at most 0.033.
Values may be sent and summed in bfloat16 or wider, within the bound.
A program may use at most 192 MiB of HBM per device.

v0:
```python
import math

import jax
import jax.numpy as jnp
from jax import lax
from jax.sharding import PartitionSpec as P

HEAD_DIM = 128


def shifted(value, axis, by):
    count = lax.axis_size(axis)
    pairs = [(i, i + by) for i in range(count) if 0 <= i + by < count]
    return lax.ppermute(value, axis, pairs)


def rotate(field, positions):
    half = field.shape[-1] // 2
    freqs = 500000.0 ** (-jnp.arange(half, dtype=jnp.float32) * 2.0 / field.shape[-1])
    angles = positions.astype(jnp.float32)[:, None] * freqs[None, :]
    cosine = jnp.cos(angles)[:, None, :]
    sine = jnp.sin(angles)[:, None, :]
    first = field[..., :half]
    second = field[..., half:]
    return jnp.concatenate(
        [first * cosine - second * sine, second * cosine + first * sine], axis=-1
    )


def normalize(block, scale_row):
    return (
        block * lax.rsqrt(jnp.mean(block * block, axis=-1, keepdims=True) + 1e-05) * scale_row
    ).astype(jnp.bfloat16)


def per_device(tokens, norm_gain, query_weight, keyval_weight, output_weight):
    segments = lax.axis_size("pipe")
    segment = lax.axis_index("pipe")
    tp_size = lax.axis_size("tp")
    ctx_pos = lax.axis_index("ctx")
    micro, rows, width = tokens.shape
    span = rows * tp_size
    scale_row = norm_gain[0].astype(jnp.float32)
    full_query, full_output = (
        lax.all_gather(query_weight[0], "ctx", axis=0, tiled=True),
        lax.all_gather(output_weight[0], "ctx", axis=1, tiled=True),
    )
    keyval = keyval_weight[0]
    q_count = full_query.shape[1] // HEAD_DIM
    kv_count = keyval.shape[1] // (2 * HEAD_DIM)
    group = q_count // kv_count
    positions = ctx_pos * span + jnp.arange(span, dtype=jnp.int32)
    factor = 1.0 / math.sqrt(HEAD_DIM)
    steps = micro + segments - 1
    received = jnp.zeros_like(tokens[0])
    results = []
    for step in range(steps):
        fresh = tokens[min(step, micro - 1)]
        state = jnp.where(segment == 0, fresh, received)
        wide = state.astype(jnp.float32)
        layer_normed = lax.all_gather(normalize(wide, scale_row), "tp", axis=0, tiled=True)
        query = jnp.dot(layer_normed, full_query, preferred_element_type=jnp.float32).reshape(
            span, q_count, HEAD_DIM
        )
        query = rotate(query, positions).astype(jnp.bfloat16)
        query = query.reshape(span, kv_count, group, HEAD_DIM).transpose(1, 2, 0, 3)
        projected = jnp.dot(layer_normed, keyval, preferred_element_type=jnp.float32).reshape(
            span, kv_count, 2, HEAD_DIM
        )
        keys = (
            rotate(projected[:, :, 0], positions)
            .astype(jnp.bfloat16)
            .reshape(span, kv_count * HEAD_DIM)
        )
        values = projected[:, :, 1].astype(jnp.bfloat16).reshape(span, kv_count * HEAD_DIM)
        piece = (
            lax.all_gather(keys, "ctx", axis=0, tiled=True),
            lax.all_gather(values, "ctx", axis=0, tiled=True),
        )
        run_max = jnp.full((kv_count, group, span), -1e30, jnp.float32)
        count = piece[0].shape[0]
        key_block = piece[0].reshape(count, kv_count, HEAD_DIM)
        value_block = piece[1].reshape(count, kv_count, HEAD_DIM)
        scores = (
            jnp.einsum("hgqd,khd->hgqk", query, key_block, preferred_element_type=jnp.float32)
            * factor
        )
        key_pos = jnp.arange(count, dtype=jnp.int32)
        allowed = key_pos[None, :] <= positions[:, None]
        scores = jnp.where(allowed, scores, -jnp.inf)
        new_max = jnp.maximum(run_max, jnp.max(scores, axis=-1))
        weights = jnp.exp(scores - new_max[..., None])
        total = jnp.sum(weights, axis=-1)
        mixed = jnp.einsum(
            "hgqk,khd->hgqd",
            weights.astype(jnp.bfloat16),
            value_block,
            preferred_element_type=jnp.float32,
        )
        run_max = new_max
        run_acc = mixed
        mixed = run_acc / total[..., None]
        attended = (
            mixed.transpose(2, 0, 1, 3).reshape(span, q_count * HEAD_DIM).astype(jnp.bfloat16)
        )
        summed = lax.psum_scatter(
            jnp.dot(attended, full_output, preferred_element_type=jnp.float32).astype(jnp.bfloat16),
            "tp",
            scatter_dimension=0,
            tiled=True,
        ).astype(jnp.float32)
        produced = (wide + summed).astype(jnp.bfloat16)
        results.append(produced)
        if step + 1 < steps:
            received = shifted(produced, "pipe", 1)
    stacked = jnp.stack(results)
    mine = lax.dynamic_slice_in_dim(stacked, segment, micro, 0)
    return mine[None]


def solution(mesh):
    in_specs = (
        P(None, ("ctx", "tp"), None),
        P("pipe", None),
        P("pipe", "ctx", "tp"),
        P("pipe", None, "tp"),
        P("pipe", "tp", "ctx"),
    )
    out_specs = P("pipe", None, ("ctx", "tp"), None)
    return jax.shard_map(
        per_device, mesh=mesh, in_specs=in_specs, out_specs=out_specs, check_vma=False
    )
```

profile of v0, /device:TPU:0, one launch (start us, length us, event | category | flops | bytes accessed | tf_op | source)
XLA Modules:
  0.0 757.9 jit_solution(15339025469367962142)
XLA Ops:
  6.5 0.7 mul.237
  7.3 1.3 fusion.38
  8.6 2.0 fusion.40
  10.7 0.7 all-gather.23.cloned.1.call-update
  11.4 11.3 %copy.36 = bf16[1024,4096]{1,0:T(8,128)(2,1)} copy(bf16[1024,4096]{0,1:T(8,128)(2,1)} %bitcast.124) | data formatting | bytes 16777216 | tf_op jit(solution)/shard_map/dot_general | solution.py:67
  22.7 0.2 multiply_cosine_fusion
  22.9 11.9 %all-gather.11.cloned.1.call-done = bf16[128,4096]{1,0:T(8,128)(2,1)} async-done(((bf16[64,4096]{1,0:T(8,128)(2,1)}), bf16[128,4096]{1,0:T(8,128)(2,1)}) %all-gather.11.cloned.1.call-update) | async-done | bytes 1048592 | tf_op jit(solution)/shard_map/all_gather | solution.py:61
  34.8 6.1 fusion.48
  41.0 0.7 pad_maximum_fusion
  41.7 0.7 slice.83
  42.5 0.5 all-gather.25.cloned.1.call-update
  43.0 0.2 reduce-scatter.3.cloned.1.call-start
  43.6 220.6 %all-gather.23.cloned.1.call-done = bf16[1,4096,2048]{2,1,0:T(8,128)(2,1)} async-done(((bf16[1,512,2048]{2,1,0:T(8,128)(2,1)}), bf16[1,4096,2048]{2,1,0:T(8,128)(2,1)}) %all-gather.23.cloned.1.call-update) | async-done | bytes 16777232 | tf_op jit(solution)/shard_map/all_gather | solution.py:45
  264.2 8.1 %fusion.32 = f32[16,8,16,128]{3,1,2,0:T(8,128)S(1)} fusion(bf16[128,4096]{1,0:T(8,128)(2,1)S(1)} %copy-done.3, bf16[1,4096,2048]{2,1,0:T(8,128)(2,1)} %all-gather.23.cloned.1.call-done), kind=kOutput, calls=%fused_computation.32 | convolution fusion | flops 2147483648 | bytes 18874368 | tf_op jit(solution)/shard_map/dot_general | solution.py:62
  272.3 0.2 copy.38
  272.5 0.5 subtract_convert_fusion.1
  273.4 30.5 %all-gather.13.cloned.1.call-done = bf16[1024,512]{0,1:T(8,128)(2,1)} async-done(((bf16[128,512]{0,1:T(8,128)(2,1)}), bf16[1024,512]{0,1:T(8,128)(2,1)}) %all-gather.13.cloned.1.call-update) | async-done | bytes 1048592 | tf_op jit(solution)/shard_map/all_gather | solution.py:77
  303.9 3.1 fusion.8
  307.0 3.2 copy-done.1
  310.2 2.3 fusion.10
  312.5 31.8 %all-gather.15.cloned.1.call-done = bf16[1024,512]{0,1:T(8,128)(2,1)} async-done(((bf16[128,512]{0,1:T(8,128)(2,1)}), bf16[1024,512]{0,1:T(8,128)(2,1)}) %all-gather.15.cloned.1.call-update) | async-done | bytes 1048592 | tf_op jit(solution)/shard_map/all_gather | solution.py:78
  344.2 5.8 divide_convert_fusion.1
  350.0 222.5 %all-gather.25.cloned.1.call-done = bf16[1,2048,4096]{2,1,0:T(8,128)(2,1)} async-done(((bf16[1,2048,512]{2,1,0:T(8,128)(2,1)}), bf16[1,2048,4096]{2,1,0:T(8,128)(2,1)}) %all-gather.25.cloned.1.call-update) | async-done | bytes 16777232 | tf_op jit(solution)/shard_map/all_gather | solution.py:46
  572.5 9.2 %fusion.14 = bf16[128,4096]{1,0:T(8,128)(2,1)} fusion(bf16[128,2048]{0,1:T(8,128)(2,1)S(1)} %bitcast.132, bf16[1,2048,4096]{2,1,0:T(8,128)(2,1)} %all-gather.25.cloned.1.call-done), kind=kOutput, calls=%fused_computation.18 | convolution fusion | flops 2148007936 | bytes 18350080 | tf_op jit(solution)/shard_map/dot_general | solution.py:107
  581.7 18.7 %reduce-scatter.3.cloned.1.call-done = bf16[64,4096]{1,0:T(8,128)(2,1)} async-done(((bf16[128,4096]{1,0:T(8,128)(2,1)}), bf16[64,4096]{1,0:T(8,128)(2,1)}) %reduce-scatter.3.cloned.1.call-update) | async-done | bytes 524304 | tf_op jit(solution)/shard_map/reduce_scatter | solution.py:106
  600.4 1.2 fusion.41
  601.6 1.6 collective-permute-start
  603.2 1.5 collective-permute-done
  604.7 0.3 fusion.42
  605.0 1.0 fusion.44
  606.0 0.3 all-gather.19.cloned.1.call-start
  606.3 21.2 %all-gather.17.cloned.1.call-done = bf16[128,4096]{1,0:T(8,128)(2,1)} async-done(((bf16[64,4096]{1,0:T(8,128)(2,1)}), bf16[128,4096]{1,0:T(8,128)(2,1)}) %all-gather.17.cloned.1.call-update) | async-done | bytes 1048592 | tf_op jit(solution)/shard_map/all_gather | solution.py:61
  627.5 6.1 fusion.46
  633.7 0.7 pad_maximum_fusion.1
  634.4 0.7 slice.82
  635.2 8.1 %fusion.35 = f32[16,8,16,128]{3,1,2,0:T(8,128)S(1)} fusion(bf16[128,4096]{1,0:T(8,128)(2,1)S(1)} %copy-done.4, bf16[1,4096,2048]{2,1,0:T(8,128)(2,1)} %all-gather.23.cloned.1.call-done), kind=kOutput, calls=%fused_computation.33 | convolution fusion | flops 2147483648 | bytes 18874368 | tf_op jit(solution)/shard_map/dot_general | solution.py:62
  643.3 0.2 copy.39
  643.5 0.5 subtract_convert_fusion
  644.3 29.6 %all-gather.19.cloned.1.call-done = bf16[1024,512]{0,1:T(8,128)(2,1)} async-done(((bf16[128,512]{0,1:T(8,128)(2,1)}), bf16[1024,512]{0,1:T(8,128)(2,1)}) %all-gather.19.cloned.1.call-update) | async-done | bytes 1048592 | tf_op jit(solution)/shard_map/all_gather | solution.py:77
  673.9 3.1 fusion.9
  677.1 3.2 copy-done
  680.3 2.3 fusion.12
  682.5 31.9 %all-gather.21.cloned.1.call-done = bf16[1024,512]{0,1:T(8,128)(2,1)} async-done(((bf16[128,512]{0,1:T(8,128)(2,1)}), bf16[1024,512]{0,1:T(8,128)(2,1)}) %all-gather.21.cloned.1.call-update) | async-done | bytes 1048592 | tf_op jit(solution)/shard_map/all_gather | solution.py:78
  714.4 5.8 divide_convert_fusion
  720.2 9.1 %fusion.17 = bf16[128,4096]{1,0:T(8,128)(2,1)} fusion(bf16[128,2048]{0,1:T(8,128)(2,1)S(1)} %bitcast.133, bf16[1,2048,4096]{2,1,0:T(8,128)(2,1)} %all-gather.25.cloned.1.call-done), kind=kOutput, calls=%fused_computation.19 | convolution fusion | flops 2148007936 | bytes 18350080 | tf_op jit(solution)/shard_map/dot_general | solution.py:107
  729.3 19.6 %reduce-scatter.5.cloned.1.call-done = bf16[64,4096]{1,0:T(8,128)(2,1)} async-done(((bf16[128,4096]{1,0:T(8,128)(2,1)}), bf16[64,4096]{1,0:T(8,128)(2,1)}) %reduce-scatter.5.cloned.1.call-update) | async-done | bytes 524304 | tf_op jit(solution)/shard_map/reduce_scatter | solution.py:106
  748.9 1.2 fusion.56
  750.0 1.0 fusion.55
  (42 shorter events, 1.5 us)
Async XLA Ops:
  6.5 28.2 %all-gather.11.cloned.1.call-start = ((), (), s32[]{:S(2)}) async-start(), calls=%async_computation.2 | async-start | bytes 1572864 | tf_op jit(solution)/shard_map/all_gather | solution.py:61
  10.6 253.6 %all-gather.23.cloned.1.call-start = ((), (), s32[]{:S(2)}) async-start(), calls=%async_computation.10 | async-start | bytes 18874368 | tf_op jit(solution)/shard_map/all_gather | solution.py:45
  11.4 292.5 %all-gather.13.cloned.1.call-start = ((), (), s32[]{:S(2)}) async-start(), calls=%async_computation.3 | async-start | bytes 1179648 | tf_op jit(solution)/shard_map/all_gather | solution.py:77
  34.8 229.4 %copy-start.3 = (bf16[128,4096]{1,0:T(8,128)(2,1)S(1)}, bf16[128,4096]{1,0:T(8,128)(2,1)}, u32[]{:S(2)}) copy-start(bf16[128,4096]{1,0:T(8,128)(2,1)} %all-gather.11.cloned.1.call-done) | copy-start | bytes 3145732
  41.7 302.6 %all-gather.15.cloned.1.call-start = ((), (), s32[]{:S(2)}) async-start(), calls=%async_computation.4 | async-start | bytes 1179648 | tf_op jit(solution)/shard_map/all_gather | solution.py:78
  42.4 530.0 %all-gather.25.cloned.1.call-start = ((), (), s32[]{:S(2)}) async-start(), calls=%async_computation.11 | async-start | bytes 18874368 | tf_op jit(solution)/shard_map/all_gather | solution.py:46
  43.0 557.4 %reduce-scatter.3.cloned.1.call-start = ((), (), s32[]{:S(2)}) async-start(), calls=%async_computation.5 | async-start | bytes 1572864 | tf_op jit(solution)/shard_map/reduce_scatter | solution.py:106
  307.0 3.2 copy-start.1
  572.5 28.0 %copy-start.2 = (bf16[1,64,4096]{2,1,0:T(8,128)(2,1)S(1)}, bf16[1,64,4096]{2,1,0:T(8,128)(2,1)}, u32[]{:S(2)}) copy-start(bf16[1,64,4096]{2,1,0:T(8,128)(2,1)} %param.5) | copy-start | bytes 1572868
  581.7 45.8 %all-gather.17.cloned.1.call-start = ((), (), s32[]{:S(2)}) async-start(), calls=%async_computation.6 | async-start | bytes 1572864 | tf_op jit(solution)/shard_map/all_gather | solution.py:61
  601.6 3.1 collective-permute-start
  606.0 67.9 %all-gather.19.cloned.1.call-start = ((), (), s32[]{:S(2)}) async-start(), calls=%async_computation.7 | async-start | bytes 1179648 | tf_op jit(solution)/shard_map/all_gather | solution.py:77
  627.5 7.7 %copy-start.4 = (bf16[128,4096]{1,0:T(8,128)(2,1)S(1)}, bf16[128,4096]{1,0:T(8,128)(2,1)}, u32[]{:S(2)}) copy-start(bf16[128,4096]{1,0:T(8,128)(2,1)} %all-gather.17.cloned.1.call-done) | copy-start | bytes 3145732
  634.4 80.0 %all-gather.21.cloned.1.call-start = ((), (), s32[]{:S(2)}) async-start(), calls=%async_computation.8 | async-start | bytes 1179648 | tf_op jit(solution)/shard_map/all_gather | solution.py:78
  635.1 113.8 %reduce-scatter.5.cloned.1.call-start = ((), (), s32[]{:S(2)}) async-start(), calls=%async_computation.9 | async-start | bytes 1572864 | tf_op jit(solution)/shard_map/reduce_scatter | solution.py:106
  677.0 3.2 copy-start
Sparse Core Ops, SparseCore 0:
  10.7 23.9 all-gather.10
  36.9 227.2 all-gather.22
  266.3 37.5 all-gather.12
  305.8 38.3 all-gather.14
  346.1 226.3 all-gather.24
  581.8 18.5 reduce-scatter.2
  606.1 21.2 all-gather.16
  634.5 39.3 all-gather.18
  676.0 38.3 all-gather.20
  729.4 19.3 reduce-scatter.4
where the time goes:
time: 759 us; the launch traced here: 758 us
  waiting for transfers between devices  641 us (84%)
  matrix products  64.4 us (8%)
  local copies, waits for them, and re-layouts  20.2 us (3%)
  other arithmetic  16.1 us (2%)
  between operations  13.8 us (2%)
    all_gather x1, waiting for transfers between devices, per_device(): lax.all_gather(output_weight[0], 'ctx', axis=1, tiled=True)  222 us
    all_gather x1, waiting for transfers between devices, per_device(): lax.all_gather(query_weight[0], 'ctx', axis=0, tiled=True)  221 us
    all_gather x2, waiting for transfers between devices, per_device(): lax.all_gather(values, 'ctx', axis=0, tiled=True)  63.6 us
    all_gather x2, waiting for transfers between devices, per_device(): lax.all_gather(keys, 'ctx', axis=0, tiled=True)  60.1 us
    reduce_scatter x2, waiting for transfers between devices, per_device(): lax.psum_scatter(jnp.dot(attended, full_output, preferred_element_type=jn...  38.2 us
    all_gather x2, waiting for transfers between devices, per_device(): lax.all_gather(normalize(wide, scale_row), 'tp', axis=0, tiled=True)  33.1 us
    dot_general x2, matrix products, per_device(): jnp.dot(attended, full_output, preferred_element_type=jnp.float32)  18.3 us
    dot_general x2, matrix products, per_device(): jnp.dot(layer_normed, full_query, preferred_element_type=jnp.float32)  16.2 us
  transfers between devices with their start and end apart: 11, of which 11 were waited for; matrix products, arithmetic and copies ran while one was open for 7% of the time, Pallas kernels for 0%

commit v1 on v0

--- a/solution.py
+++ b/solution.py
@@ -33,7 +33,7 @@
     ).astype(jnp.bfloat16)
 
 
-def per_device(tokens, norm_gain, query_weight, keyval_weight, output_weight):
+def gathered(tokens, norm_gain, query_weight, keyval_weight, output_weight):
     segments = lax.axis_size("pipe")
     segment = lax.axis_index("pipe")
     tp_size = lax.axis_size("tp")
@@ -118,6 +118,102 @@
     return mine[None]
 
 
+def swap_halves(weight, axis):
+    segments = lax.axis_size("pipe")
+    shape = weight.shape
+    split = shape[:axis] + (segments, shape[axis] // segments) + shape[axis + 1 :]
+    blocks = jnp.moveaxis(weight.reshape(split), axis, 0)
+    return lax.all_to_all(blocks, "pipe", 0, 0)
+
+
+def attend(query, keys, values, positions):
+    span, q_count, _ = query.shape
+    kv_count = keys.shape[1]
+    group = q_count // kv_count
+    query = query.reshape(span, kv_count, group, HEAD_DIM).transpose(1, 2, 0, 3)
+    scores = jnp.einsum("hgqd,khd->hgqk", query, keys, preferred_element_type=jnp.float32)
+    scores = scores * (1.0 / math.sqrt(HEAD_DIM))
+    allowed = jnp.arange(keys.shape[0], dtype=jnp.int32)[None, :] <= positions[:, None]
+    scores = jnp.where(allowed, scores, -jnp.inf)
+    weights = jnp.exp(scores - jnp.max(scores, axis=-1, keepdims=True))
+    total = jnp.sum(weights, axis=-1, keepdims=True)
+    mixed = jnp.einsum(
+        "hgqk,khd->hgqd",
+        weights.astype(jnp.bfloat16),
+        values,
+        preferred_element_type=jnp.float32,
+    )
+    mixed = (mixed / total).astype(jnp.bfloat16)
+    return mixed.transpose(2, 0, 1, 3).reshape(span, q_count * HEAD_DIM)
+
+
+def spread(tokens, norm_gain, query_weight, keyval_weight, output_weight):
+    layers = lax.axis_size("pipe")
+    tp_size = lax.axis_size("tp")
+    ctx_size = lax.axis_size("ctx")
+    part = lax.axis_index("pipe")
+    ctx_pos = lax.axis_index("ctx")
+    micro, rows, width = tokens.shape
+    mine = rows // layers
+    span = rows * tp_size
+    slab = width // ctx_size
+    gains = lax.all_gather(norm_gain[0], "pipe", axis=0)
+    kv_rows = lax.dynamic_slice_in_dim(keyval_weight[0], ctx_pos * slab, slab, 0)
+    project = swap_halves(query_weight[0], 1)
+    kv_project = swap_halves(kv_rows, 1)
+    q_cols = project.shape[2]
+    project = jnp.concatenate([project, kv_project], axis=2)
+    combine = swap_halves(output_weight[0], 0)
+    kv_count = kv_project.shape[2] // (2 * HEAD_DIM)
+    q_count = q_cols // HEAD_DIM
+    positions = ctx_pos * span + jnp.arange(span, dtype=jnp.int32)
+    outs = []
+    for m in range(micro):
+        state = lax.dynamic_slice_in_dim(tokens[m], part * mine, mine, 0)
+        produced = []
+        for layer in range(layers):
+            wide = state.astype(jnp.float32)
+            normed = normalize(wide, gains[layer].astype(jnp.float32))
+            sliced = lax.all_to_all(normed.reshape(mine, ctx_size, slab), "ctx", 1, 0)
+            sliced = sliced.reshape(ctx_size, mine, slab)
+            everyone = lax.all_gather(sliced, ("tp", "pipe"), axis=1, tiled=True)
+            everyone = everyone.reshape(ctx_size * span, slab)
+            partial = jnp.dot(everyone, project[layer], preferred_element_type=jnp.float32)
+            projected = lax.psum_scatter(
+                partial.astype(jnp.bfloat16), "ctx", scatter_dimension=0, tiled=True
+            ).astype(jnp.float32)
+            query = rotate(projected[:, :q_cols].reshape(span, q_count, HEAD_DIM), positions)
+            kv = projected[:, q_cols:].reshape(span, kv_count, 2, HEAD_DIM)
+            kv = jnp.stack([rotate(kv[:, :, 0], positions), kv[:, :, 1]], axis=2)
+            kv = lax.all_gather(
+                kv.astype(jnp.bfloat16).reshape(span, kv_count * 2 * HEAD_DIM),
+                "ctx",
+                axis=0,
+                tiled=True,
+            ).reshape(ctx_size * span, kv_count, 2, HEAD_DIM)
+            attended = attend(query.astype(jnp.bfloat16), kv[:, :, 0], kv[:, :, 1], positions)
+            attended = lax.all_gather(attended, "ctx", axis=0, tiled=True)
+            partial = jnp.dot(attended, combine[layer], preferred_element_type=jnp.float32)
+            partial = partial.astype(jnp.bfloat16).reshape(ctx_size, span, slab)
+            summed = lax.psum_scatter(
+                partial, ("tp", "pipe"), scatter_dimension=1, tiled=True
+            )
+            summed = lax.all_to_all(summed, "ctx", 0, 1)
+            summed = summed.reshape(mine, width).astype(jnp.float32)
+            state = (wide + summed).astype(jnp.bfloat16)
+            produced.append(state)
+        outs.append(lax.all_to_all(jnp.stack(produced), "pipe", 0, 0).reshape(rows, width))
+    return jnp.stack(outs)[None]
+
+
+def per_device(tokens, norm_gain, query_weight, keyval_weight, output_weight):
+    layers = lax.axis_size("pipe")
+    kv_count = keyval_weight.shape[2] // (2 * HEAD_DIM)
+    even = kv_count % layers == 0 and tokens.shape[1] % (16 * layers) == 0
+    step = spread if even else gathered
+    return step(tokens, norm_gain, query_weight, keyval_weight, output_weight)
+
+
 def solution(mesh):
     in_specs = (
         P(None, ("ctx", "tp"), None),

time: 759 us -> 527 us (0.69)
  waiting for transfers between devices: 641 us -> 394 us
  blocking collectives: 0 us -> 40.8 us
  matrix products: 64.4 us -> 25.9 us
  starting transfers between devices: 2.37 us -> 19.8 us
    all_gather x8 -> x6, waiting for transfers between devices: 600 us -> 181 us  [the longest x2 92.6 us: spread(): attended = lax.all_gather(attended, 'ctx', axis=0, tiled=True)]
    reduce_scatter x2 -> x4, waiting for transfers between devices: 38.2 us -> 194 us  [the longest x2 148 us: spread(): lax.psum_scatter(partial.astype(jnp.bfloat16), 'ctx', scatter_dimension=0...]
    all_to_all x0 -> x4, blocking collectives: none -> 38.6 us  [the longest x2 28.1 us: spread(): sliced = lax.all_to_all(normed.reshape(mine, ctx_size, slab), 'ctx', 1, 0)]
    dot_general x10 -> x8, matrix products: 64.4 us -> 25.9 us  [the longest x2 9.88 us: spread(): jnp.dot(everyone, project[layer], preferred_element_type=jnp.float32)]
    all_to_all x0 -> x4, starting transfers between devices: none -> 19.3 us  [the longest x2 11 us: spread(): summed = lax.all_to_all(summed, 'ctx', 0, 1)]
    all_to_all x0 -> x4, waiting for transfers between devices: none -> 18 us  [the longest x2 17.3 us: spread(): summed = lax.all_to_all(summed, 'ctx', 0, 1)]
    dot_general x1 -> x0, local copies, waits for them, and re-layouts: 11.3 us -> none  [per_device(): jnp.dot(layer_normed, keyval, preferred_element_type=jnp.float32)]
  transfers between devices with their start and end apart: 11 -> 14, of which waited for: 11 -> 12; matrix products, arithmetic and copies ran while one was open for 7% -> 3% of each run, Pallas kernels for 0% -> 0%
where the time goes in v1:
time: 527 us; the launch traced here: 525 us
  waiting for transfers between devices  394 us (75%)
  blocking collectives  40.8 us (8%)
  matrix products  25.9 us (5%)
  local copies, waits for them, and re-layouts  22.4 us (4%)
  starting transfers between devices  19.8 us (4%)
  between operations  14 us (3%)
  other arithmetic  8.96 us (2%)
    reduce_scatter x2, waiting for transfers between devices, spread(): lax.psum_scatter(partial.astype(jnp.bfloat16), 'ctx', scatter_dimension=0...  148 us
    all_gather x2, waiting for transfers between devices, spread(): attended = lax.all_gather(attended, 'ctx', axis=0, tiled=True)  92.6 us
    all_gather x2, waiting for transfers between devices, spread(): lax.all_gather(kv.astype(jnp.bfloat16).reshape(span, kv_count * 2 * HEAD_...  73.9 us
    reduce_scatter x2, waiting for transfers between devices, spread(): lax.psum_scatter(partial, ('tp', 'pipe'), scatter_dimension=1, tiled=True)  46.3 us
    all_to_all x2, blocking collectives, spread(): sliced = lax.all_to_all(normed.reshape(mine, ctx_size, slab), 'ctx', 1, 0)  28.1 us
    all_to_all x2, waiting for transfers between devices, spread(): summed = lax.all_to_all(summed, 'ctx', 0, 1)  17.3 us
    all_gather x2, waiting for transfers between devices, spread(): everyone = lax.all_gather(sliced, ('tp', 'pipe'), axis=1, tiled=True)  14.7 us
    all_to_all x2, starting transfers between devices, spread(): summed = lax.all_to_all(summed, 'ctx', 0, 1)  11 us
  transfers between devices with their start and end apart: 14, of which 12 were waited for; matrix products, arithmetic and copies ran while one was open for 3% of the time, Pallas kernels for 0%

profile of v1, /device:TPU:0, one launch (start us, length us, event | category | flops | bytes accessed | tf_op | source)
XLA Modules:
  0.0 525.4 jit_solution(17571190641477279088)
XLA Ops:
  6.5 1.1 dynamic-slice_convert_fusion
  7.7 1.1 fusion.35
  9.1 2.2 all-gather.2
  11.6 16.2 %all_to_all.68 = bf16[1,32,8,512]{3,1,0,2:T(8,128)(2,1)S(1)} all-to-all(bf16[1,32,8,512]{3,1,0,2:T(8,128)(2,1)S(1)} %copy.76), channel_id=1, replica_groups=mesh['pipe'=2,'ctx'=8,'tp'=2] {'ctx'}, dimensions={2} | all-to-all | bytes 524288 | tf_op jit(solution)/shard_map/all_to_all | solution.py:177
  27.8 0.9 copy.77
  28.7 2.5 copy.79
  31.2 3.8 all-to-all-start.1
  35.0 2.3 constant_dynamic-slice_fusion
  37.3 2.3 copy.106
  39.6 4.4 all-to-all-start.2
  44.1 1.5 constant_dynamic-update-slice_fusion.1
  46.3 2.3 constant_dynamic-update-slice_fusion
  48.6 1.5 copy.78
  50.1 4.9 convolution_convert_fusion.1
  55.5 73.2 %reduce-scatter.5.cloned.1.call-done = bf16[128,1536]{1,0:T(8,128)(2,1)} async-done(((bf16[1024,1536]{1,0:T(8,128)(2,1)}), bf16[128,1536]{1,0:T(8,128)(2,1)}) %reduce-scatter.5.cloned.1.call-update) | async-done | bytes 393232 | tf_op jit(solution)/shard_map/reduce_scatter | solution.py:182
  128.7 0.9 slice.113
  130.3 0.8 copy.86
  131.3 1.1 convert_element_type.208
  132.9 36.9 %all-gather.10.cloned.1.call-done = bf16[1024,512]{0,1:T(8,128)(2,1)} async-done(((bf16[128,512]{0,1:T(8,128)(2,1)}), bf16[1024,512]{0,1:T(8,128)(2,1)}) %all-gather.10.cloned.1.call-update) | async-done | bytes 1048592 | tf_op jit(solution)/shard_map/all_gather | solution.py:188
  169.8 2.2 fusion
  172.0 1.1 fusion.2
  173.1 1.9 fusion.27
  175.0 6.3 %all_to_all.69 = bf16[2,1024,512]{2,1,0:T(8,128)(2,1)} all-to-all(bf16[2,1024,512]{2,1,0:T(8,128)(2,1)S(1)} %bitcast.183), channel_id=1, replica_groups=mesh['pipe'=2,'ctx'=8,'tp'=2] {'pipe'}, dimensions={0} | all-to-all | bytes 4194304 | tf_op jit(solution)/shard_map/all_to_all | solution.py:126
  181.3 43.2 %all-gather.12.cloned.1.call-done = bf16[1024,1024]{0,1:T(8,128)(2,1)} async-done(((bf16[128,1024]{0,1:T(8,128)(2,1)}), bf16[1024,1024]{0,1:T(8,128)(2,1)}) %all-gather.12.cloned.1.call-update) | async-done | bytes 2097168 | tf_op jit(solution)/shard_map/all_gather | solution.py:195
  224.5 4.1 convolution_convert_fusion.3
  228.7 23.2 %reduce-scatter.7.cloned.1.call-done = bf16[8,32,512]{2,1,0:T(8,128)(2,1)} async-done(((bf16[8,128,512]{2,1,0:T(8,128)(2,1)}), bf16[8,32,512]{2,1,0:T(8,128)(2,1)}) %reduce-scatter.7.cloned.1.call-update) | async-done | bytes 262160 | tf_op jit(solution)/shard_map/reduce_scatter | solution.py:198
  251.8 5.5 %all-to-all-start.4 = ((bf16[8,32,1,512]{3,1,2,0:T(8,128)(2,1)}), bf16[8,32,1,512]{3,1,2,0:T(8,128)(2,1)S(1)}, u32[]{:S(2)}, u32[]{:S(2)}) async-start(bf16[8,32,1,512]{3,1,2,0:T(8,128)(2,1)} %bitcast.206), calls=%async_computation.6 | async-start | bytes 524288 | tf_op jit(solution)/shard_map/all_to_all | solution.py:201
  257.4 8.7 %all-to-all-done.4 = bf16[8,32,1,512]{3,1,2,0:T(8,128)(2,1)S(1)} async-done(((bf16[8,32,1,512]{3,1,2,0:T(8,128)(2,1)}), bf16[8,32,1,512]{3,1,2,0:T(8,128)(2,1)S(1)}, u32[]{:S(2)}, u32[]{:S(2)}) %all-to-all-start.4) | async-done | bytes 262176 | tf_op jit(solution)/shard_map/all_to_all | solution.py:201
  267.1 12.0 %all_to_all.70 = bf16[1,32,8,512]{3,1,0,2:T(8,128)(2,1)S(1)} all-to-all(bf16[1,32,8,512]{3,1,0,2:T(8,128)(2,1)S(1)} %copy.90), channel_id=1, replica_groups=mesh['pipe'=2,'ctx'=8,'tp'=2] {'ctx'}, dimensions={2} | all-to-all | bytes 524288 | tf_op jit(solution)/shard_map/all_to_all | solution.py:177
  279.0 0.9 copy.91
  280.2 14.7 %all-gather.20.cloned.1.call-done = bf16[8,1,128,1,512]{4,0,3,1,2:T(8,128)(2,1)} async-done(((bf16[8,1,32,1,512]{4,0,3,1,2:T(8,128)(2,1)}), bf16[8,1,128,1,512]{4,0,3,1,2:T(8,128)(2,1)}) %all-gather.20.cloned.1.call-update) | async-done | bytes 1048592 | tf_op jit(solution)/shard_map/all_gather | solution.py:179
  294.9 1.5 copy.92
  296.4 4.9 convolution_convert_fusion
  301.4 74.6 %reduce-scatter.9.cloned.1.call-done = bf16[128,1536]{1,0:T(8,128)(2,1)} async-done(((bf16[1024,1536]{1,0:T(8,128)(2,1)}), bf16[128,1536]{1,0:T(8,128)(2,1)}) %reduce-scatter.9.cloned.1.call-update) | async-done | bytes 393232 | tf_op jit(solution)/shard_map/reduce_scatter | solution.py:182
  376.0 0.9 slice.126
  377.6 0.8 copy.98
  378.5 1.1 convert_element_type.230
  380.1 37.0 %all-gather.14.cloned.1.call-done = bf16[1024,512]{0,1:T(8,128)(2,1)} async-done(((bf16[128,512]{0,1:T(8,128)(2,1)}), bf16[1024,512]{0,1:T(8,128)(2,1)}) %all-gather.14.cloned.1.call-update) | async-done | bytes 1048592 | tf_op jit(solution)/shard_map/all_gather | solution.py:188
  417.0 2.1 fusion.1
  419.2 1.1 fusion.4
  420.3 1.9 fusion.21
  422.3 49.5 %all-gather.16.cloned.1.call-done = bf16[1024,1024]{0,1:T(8,128)(2,1)} async-done(((bf16[128,1024]{0,1:T(8,128)(2,1)}), bf16[1024,1024]{0,1:T(8,128)(2,1)}) %all-gather.16.cloned.1.call-update) | async-done | bytes 2097168 | tf_op jit(solution)/shard_map/all_gather | solution.py:195
  471.7 3.8 convolution_convert_fusion.2
  475.6 23.2 %reduce-scatter.11.cloned.1.call-done = bf16[8,32,512]{2,1,0:T(8,128)(2,1)} async-done(((bf16[8,128,512]{2,1,0:T(8,128)(2,1)}), bf16[8,32,512]{2,1,0:T(8,128)(2,1)}) %reduce-scatter.11.cloned.1.call-update) | async-done | bytes 262160 | tf_op jit(solution)/shard_map/reduce_scatter | solution.py:198
  498.8 5.5 %all-to-all-start.6 = ((bf16[8,32,1,512]{3,1,2,0:T(8,128)(2,1)}), bf16[8,32,1,512]{3,1,2,0:T(8,128)(2,1)S(1)}, u32[]{:S(2)}, u32[]{:S(2)}) async-start(bf16[8,32,1,512]{3,1,2,0:T(8,128)(2,1)} %bitcast.207), calls=%async_computation.10 | async-start | bytes 524288 | tf_op jit(solution)/shard_map/all_to_all | solution.py:201
  504.4 8.7 %all-to-all-done.6 = bf16[8,32,1,512]{3,1,2,0:T(8,128)(2,1)S(1)} async-done(((bf16[8,32,1,512]{3,1,2,0:T(8,128)(2,1)}), bf16[8,32,1,512]{3,1,2,0:T(8,128)(2,1)S(1)}, u32[]{:S(2)}, u32[]{:S(2)}) %all-to-all-start.6) | async-done | bytes 262176 | tf_op jit(solution)/shard_map/all_to_all | solution.py:201
  513.7 4.2 all_to_all.71
  517.8 0.8 copy.132
  (87 shorter events, 6.4 us)
Async XLA Ops:
  6.5 22.1 %copy-start = (bf16[1,512,2048]{2,1,0:T(8,128)(2,1)S(1)}, bf16[1,512,2048]{2,1,0:T(8,128)(2,1)}, u32[]{:S(2)}) copy-start(bf16[1,512,2048]{2,1,0:T(8,128)(2,1)} %param.7) | copy-start | bytes 6291460
  6.5 42.0 %all-gather.18.cloned.1.call-start = ((), (), s32[]{:S(2)}) async-start(), calls=%async_computation.20 | async-start | bytes 1310720 | tf_op jit(solution)/shard_map/all_gather | solution.py:179
  31.2 8.4 %all-to-all-start.1 = ((bf16[2,512,1024]{1,2,0:T(8,128)(2,1)}), bf16[2,512,1024]{1,2,0:T(8,128)(2,1)S(1)}, u32[]{:S(2)}, u32[]{:S(2)}) async-start(bf16[2,512,1024]{1,2,0:T(8,128)(2,1)} %bitcast.177), calls=%async_computation.1 | async-start | bytes 4194304 | tf_op jit(solution)/shard_map/all_to_all | solution.py:126
  39.6 6.7 %all-to-all-start.2 = ((bf16[2,512,512]{1,2,0:T(8,128)(2,1)}), bf16[2,512,512]{1,2,0:T(8,128)(2,1)}, u32[]{:S(2)}, u32[]{:S(2)}) async-start(bf16[2,512,512]{1,2,0:T(8,128)(2,1)} %bitcast.182), calls=%async_computation.2 | async-start | bytes 2097152 | tf_op jit(solution)/shard_map/all_to_all | solution.py:126
  44.1 84.6 %reduce-scatter.5.cloned.1.call-start = ((), (), s32[]{:S(2)}) async-start(), calls=%async_computation.12 | async-start | bytes 3538944 | tf_op jit(solution)/shard_map/reduce_scatter | solution.py:182
  55.1 114.7 %all-gather.10.cloned.1.call-start = ((), (), s32[]{:S(2)}) async-start(), calls=%async_computation.13 | async-start | bytes 1179648 | tf_op jit(solution)/shard_map/all_gather | solution.py:188
  131.1 93.4 %all-gather.12.cloned.1.call-start = ((), (), s32[]{:S(2)}) async-start(), calls=%async_computation.14 | async-start | bytes 2359296 | tf_op jit(solution)/shard_map/all_gather | solution.py:195
  169.8 3.3 copy-start.5
  173.1 2.0 copy-start.1
  175.0 76.8 %reduce-scatter.7.cloned.1.call-start = ((), (), s32[]{:S(2)}) async-start(), calls=%async_computation.15 | async-start | bytes 1310720 | tf_op jit(solution)/shard_map/reduce_scatter | solution.py:198
  181.3 85.3 %copy-start.3 = (bf16[1,64,4096]{2,1,0:T(8,128)(2,1)S(1)}, bf16[1,64,4096]{2,1,0:T(8,128)(2,1)}, u32[]{:S(2)}) copy-start(bf16[1,64,4096]{2,1,0:T(8,128)(2,1)} %param.5) | copy-start | bytes 1572868
  251.8 14.3 %all-to-all-start.4 = ((bf16[8,32,1,512]{3,1,2,0:T(8,128)(2,1)}), bf16[8,32,1,512]{3,1,2,0:T(8,128)(2,1)S(1)}, u32[]{:S(2)}, u32[]{:S(2)}) async-start(bf16[8,32,1,512]{3,1,2,0:T(8,128)(2,1)} %bitcast.206), calls=%async_computation.6 | async-start | bytes 524288 | tf_op jit(solution)/shard_map/all_to_all | solution.py:201
  257.3 37.5 %all-gather.20.cloned.1.call-start = ((), (), s32[]{:S(2)}) async-start(), calls=%async_computation.21 | async-start | bytes 1310720 | tf_op jit(solution)/shard_map/all_gather | solution.py:179
  279.9 96.1 %reduce-scatter.9.cloned.1.call-start = ((), (), s32[]{:S(2)}) async-start(), calls=%async_computation.16 | async-start | bytes 3538944 | tf_op jit(solution)/shard_map/reduce_scatter | solution.py:182
  301.3 115.7 %all-gather.14.cloned.1.call-start = ((), (), s32[]{:S(2)}) async-start(), calls=%async_computation.17 | async-start | bytes 1179648 | tf_op jit(solution)/shard_map/all_gather | solution.py:188
  378.4 93.3 %all-gather.16.cloned.1.call-start = ((), (), s32[]{:S(2)}) async-start(), calls=%async_computation.18 | async-start | bytes 2359296 | tf_op jit(solution)/shard_map/all_gather | solution.py:195
  417.0 3.3 copy-start.6
  420.3 51.4 %copy-start.2 = (bf16[2,1024,512]{2,1,0:T(8,128)(2,1)S(1)}, bf16[2,1024,512]{2,1,0:T(8,128)(2,1)}, u32[]{:S(2)}) copy-start(bf16[2,1024,512]{2,1,0:T(8,128)(2,1)} %all_to_all.69) | copy-start | bytes 6291460
  422.2 76.6 %reduce-scatter.11.cloned.1.call-start = ((), (), s32[]{:S(2)}) async-start(), calls=%async_computation.19 | async-start | bytes 1310720 | tf_op jit(solution)/shard_map/reduce_scatter | solution.py:198
  475.6 37.9 %copy-start.4 = (bf16[1,64,4096]{2,1,0:T(8,128)(2,1)S(1)}, bf16[1,64,4096]{2,1,0:T(8,128)(2,1)}, u32[]{:S(2)}) copy-start(bf16[1,64,4096]{2,1,0:T(8,128)(2,1)} %param.5) | copy-start | bytes 1572868
  498.8 14.3 %all-to-all-start.6 = ((bf16[8,32,1,512]{3,1,2,0:T(8,128)(2,1)}), bf16[8,32,1,512]{3,1,2,0:T(8,128)(2,1)S(1)}, u32[]{:S(2)}, u32[]{:S(2)}) async-start(bf16[8,32,1,512]{3,1,2,0:T(8,128)(2,1)} %bitcast.207), calls=%async_computation.10 | async-start | bytes 524288 | tf_op jit(solution)/shard_map/all_to_all | solution.py:201
Sparse Core Ops, SparseCore 0:
  28.8 15.7 all-gather.17
  55.2 73.4 reduce-scatter.4
  131.2 38.5 all-gather.9
  175.1 49.3 all-gather.11
  228.8 22.9 reduce-scatter.6
  280.0 14.7 all-gather.19
  301.5 74.4 reduce-scatter.8
  378.6 38.4 all-gather.13
  422.3 49.3 all-gather.15
  475.7 22.9 reduce-scatter.10

commit v2 on v1

--- a/solution.py
+++ b/solution.py
@@ -1,8 +1,11 @@
+import functools
 import math
 
 import jax
 import jax.numpy as jnp
 from jax import lax
+from jax.experimental import pallas as pl
+from jax.experimental.pallas import tpu as pltpu
 from jax.sharding import PartitionSpec as P
 
 HEAD_DIM = 128
@@ -116,6 +119,297 @@
     stacked = jnp.stack(results)
     mine = lax.dynamic_slice_in_dim(stacked, segment, micro, 0)
     return mine[None]
+
+
+MESH = pl.DeviceIdType.MESH
+
+
+def neighbours():
+    count = lax.axis_size("ctx") // 2
+    here = lax.axis_index("ctx")
+    row = here // 2
+    side = here % 2
+    return count, here, row, side, here + 1 - 2 * side
+
+
+def greet(count, here, row, partner):
+    barrier = pltpu.get_barrier_semaphore()
+    pl.semaphore_signal(barrier, inc=1, device_id={"ctx": partner}, device_id_type=MESH)
+
+    @pl.when(row + 1 < count)
+    def _():
+        pl.semaphore_signal(barrier, inc=1, device_id={"ctx": here + 2}, device_id_type=MESH)
+
+    @pl.when(row >= 1)
+    def _():
+        pl.semaphore_signal(barrier, inc=1, device_id={"ctx": here - 2}, device_id_type=MESH)
+
+    pl.semaphore_wait(barrier, 1 + (row + count - 1) // count + (2 * count - 2 - row) // count)
+
+
+def gather_kernel(cut, in_ref, out_ref, send_sem, recv_sem):
+    count, here, row, side, partner = neighbours()
+    rows = in_ref.shape[0]
+    pieces = (pl.ds(0, cut), pl.ds(cut, rows - cut))
+    greet(count, here, row, partner)
+    has_up = row + 1 < count
+    has_down = row >= 1
+
+    def copy(block, half, way, own=False):
+        target = (here + 2, here - 2, partner)[way]
+        there = out_ref.at[block, pieces[half]]
+        return pltpu.make_async_remote_copy(
+            src_ref=in_ref.at[pieces[half]] if own else there,
+            dst_ref=there,
+            send_sem=send_sem.at[block, half, way],
+            recv_sem=recv_sem.at[block, half],
+            device_id={"ctx": target},
+            device_id_type=MESH,
+        )
+
+    def arrive(block, half):
+        copy(block, half, 2).wait_recv()
+
+    sends = []
+
+    def send(cond, block, half, way, own=False):
+        sends.append((cond, block, half, way, own))
+
+        @pl.when(cond)
+        def _():
+            copy(block, half, way, own).start()
+
+    always = row >= 0
+    send(always, here, 1, 2, True)
+    for half in (1, 0):
+        send(has_up, here, half, 0, True)
+        send(has_down, here, half, 1, True)
+    send(always, here, 0, 2, True)
+    out_ref[here] = in_ref[...]
+    arrive(partner, 1)
+    send(has_up, partner, 1, 0)
+    send(has_down, partner, 1, 1)
+    for j in range(1, count):
+        below = row >= j
+        above = row + j < count
+        for half, away in ((0, 0), (1, 0), (1, 1)):
+            for near, step, way, onward in ((below, -2 * j, 0, has_up), (above, 2 * j, 1, has_down)):
+                block = (here if away == 0 else partner) + step
+
+                @pl.when(near)
+                def _():
+                    arrive(block, half)
+
+                send(jnp.logical_and(near, onward), block, half, way)
+                if half == 0:
+                    send(near, block, half, 2)
+    arrive(partner, 0)
+    for j in range(1, count):
+        for near, step in ((row >= j, -2 * j), (row + j < count, 2 * j)):
+
+            @pl.when(near)
+            def _():
+                arrive(partner + step, 0)
+
+    for cond, block, half, way, own in sends:
+
+        @pl.when(cond)
+        def _():
+            copy(block, half, way, own).wait_send()
+
+
+def ctx_gather(value, number):
+    rows, columns = value.shape
+    blocks = lax.axis_size("ctx")
+    gathered_value = pl.pallas_call(
+        functools.partial(gather_kernel, rows // 2),
+        out_shape=jax.ShapeDtypeStruct((blocks, rows, columns), value.dtype),
+        in_specs=[pl.BlockSpec(memory_space=pltpu.VMEM)],
+        out_specs=pl.BlockSpec(memory_space=pltpu.VMEM),
+        scratch_shapes=[
+            pltpu.SemaphoreType.DMA((blocks, 2, 3)),
+            pltpu.SemaphoreType.DMA((blocks, 2)),
+        ],
+        compiler_params=pltpu.CompilerParams(collective_id=number, has_side_effects=True),
+    )(value)
+    return gathered_value.reshape(blocks * rows, columns)
+
+
+def scatter_kernel(
+    cut, in_ref, out_ref, cross, sums, up_in, down_in, z_sums, z_up, z_down, z_cross, z_last,
+    x_send, x_recv, b_send, b_recv, a_send, a_recv, l_send, l_recv,
+):
+    count, here, row, side, partner = neighbours()
+    rows = in_ref.shape[1]
+    first, second = pl.ds(0, cut), pl.ds(cut, rows - cut)
+    greet(count, here, row, partner)
+    has_up = row + 1 < count
+    has_down = row >= 1
+    order = []
+    for j in range(count - 1, 0, -1):
+        order.append((row + j < count, row + j, 0))
+        order.append((row >= j, row - j, 1))
+    always = row >= 0
+
+    def remote(src, dst, send, recv, target):
+        return pltpu.make_async_remote_copy(
+            src_ref=src, dst_ref=dst, send_sem=send, recv_sem=recv,
+            device_id={"ctx": target}, device_id_type=MESH,
+        )
+
+    def over(dest):
+        return remote(
+            in_ref.at[2 * dest + 1 - side, second], cross.at[dest],
+            x_send.at[dest], x_recv.at[dest], partner,
+        )
+
+    def chain_b(dest, way):
+        return remote(
+            sums.at[dest], (up_in, down_in)[way].at[dest],
+            b_send.at[dest], b_recv.at[way, dest], (here + 2, here - 2)[way],
+        )
+
+    def chain_a(dest, way, x):
+        return remote(
+            z_sums.at[dest, x], (z_up, z_down)[way].at[dest, x],
+            a_send.at[dest, x], a_recv.at[way, dest, x], (here + 2, here - 2)[way],
+        )
+
+    last = remote(z_cross, z_last, l_send.at[0], l_recv.at[0], partner)
+
+    def wide(value):
+        return value.astype(jnp.float32)
+
+    for cond, dest, way in order + [(always, row, 0)]:
+
+        @pl.when(cond)
+        def _():
+            over(dest).start()
+
+    for cond, dest, way in order:
+        behind = (has_down, has_up)[way]
+        for x in range(2):
+
+            @pl.when(jnp.logical_and(cond, behind))
+            def _():
+                chain_a(dest, way, x).wait_recv()
+                z_sums[dest, x] = (
+                    wide(in_ref[2 * dest + x, first]) + wide((z_up, z_down)[way][dest, x])
+                ).astype(jnp.bfloat16)
+
+            @pl.when(jnp.logical_and(cond, jnp.logical_not(behind)))
+            def _():
+                z_sums[dest, x] = in_ref[2 * dest + x, first]
+
+            @pl.when(cond)
+            def _():
+                chain_a(dest, way, x).start()
+
+        @pl.when(cond)
+        def _():
+            over(dest).wait_recv()
+
+        @pl.when(jnp.logical_and(cond, behind))
+        def _():
+            chain_b(dest, way).wait_recv()
+            sums[dest] = (
+                wide(in_ref[2 * dest + side, second])
+                + wide(cross[dest])
+                + wide((up_in, down_in)[way][dest])
+            ).astype(jnp.bfloat16)
+
+        @pl.when(jnp.logical_and(cond, jnp.logical_not(behind)))
+        def _():
+            sums[dest] = (wide(in_ref[2 * dest + side, second]) + wide(cross[dest])).astype(jnp.bfloat16)
+
+        @pl.when(cond)
+        def _():
+            chain_b(dest, way).start()
+
+    @pl.when(has_down)
+    def _():
+        chain_a(row, 0, 0).wait_recv()
+        chain_a(row, 0, 1).wait_recv()
+
+    @pl.when(jnp.logical_not(has_down))
+    def _():
+        z_up[row] = jnp.zeros_like(z_up[row])
+        up_in[row] = jnp.zeros_like(up_in[row])
+
+    @pl.when(has_up)
+    def _():
+        chain_a(row, 1, 0).wait_recv()
+        chain_a(row, 1, 1).wait_recv()
+
+    @pl.when(jnp.logical_not(has_up))
+    def _():
+        z_down[row] = jnp.zeros_like(z_down[row])
+        down_in[row] = jnp.zeros_like(down_in[row])
+
+    z_cross[...] = (
+        wide(in_ref[partner, first]) + wide(z_up[row, 1 - side]) + wide(z_down[row, 1 - side])
+    ).astype(jnp.bfloat16)
+    last.start()
+    over(row).wait_recv()
+
+    @pl.when(has_down)
+    def _():
+        chain_b(row, 0).wait_recv()
+
+    @pl.when(has_up)
+    def _():
+        chain_b(row, 1).wait_recv()
+
+    out_ref[second] = (
+        wide(in_ref[here, second]) + wide(cross[row]) + wide(up_in[row]) + wide(down_in[row])
+    )
+    last.wait_recv()
+    out_ref[first] = (
+        wide(in_ref[here, first]) + wide(z_up[row, side]) + wide(z_down[row, side]) + wide(z_last[...])
+    )
+    for cond, dest, way in order + [(always, row, 0)]:
+
+        @pl.when(cond)
+        def _():
+            over(dest).wait_send()
+
+    for cond, dest, way in order:
+
+        @pl.when(cond)
+        def _():
+            chain_a(dest, way, 0).wait_send()
+            chain_a(dest, way, 1).wait_send()
+            chain_b(dest, way).wait_send()
+
+    last.wait_send()
+
+
+def ctx_scatter(partial, number):
+    blocks, rows, columns = partial.shape
+    count = blocks // 2
+    cut = rows * 3 // 8 // 16 * 16
+    rest = rows - cut
+    kind = partial.dtype
+    return pl.pallas_call(
+        functools.partial(scatter_kernel, cut),
+        out_shape=jax.ShapeDtypeStruct((rows, columns), jnp.float32),
+        in_specs=[pl.BlockSpec(memory_space=pltpu.VMEM)],
+        out_specs=pl.BlockSpec(memory_space=pltpu.VMEM),
+        scratch_shapes=[pltpu.VMEM((count, rest, columns), kind)] * 4
+        + [pltpu.VMEM((count, 2, cut, columns), kind)] * 3
+        + [pltpu.VMEM((cut, columns), kind)] * 2
+        + [
+            pltpu.SemaphoreType.DMA((count,)),
+            pltpu.SemaphoreType.DMA((count,)),
+            pltpu.SemaphoreType.DMA((count,)),
+            pltpu.SemaphoreType.DMA((2, count)),
+            pltpu.SemaphoreType.DMA((count, 2)),
+            pltpu.SemaphoreType.DMA((2, count, 2)),
+            pltpu.SemaphoreType.DMA((1,)),
+            pltpu.SemaphoreType.DMA((1,)),
+        ],
+        compiler_params=pltpu.CompilerParams(collective_id=number, has_side_effects=True),
+    )(partial)
 
 
 def swap_halves(weight, axis):
@@ -179,20 +473,17 @@
             everyone = lax.all_gather(sliced, ("tp", "pipe"), axis=1, tiled=True)
             everyone = everyone.reshape(ctx_size * span, slab)
             partial = jnp.dot(everyone, project[layer], preferred_element_type=jnp.float32)
-            projected = lax.psum_scatter(
-                partial.astype(jnp.bfloat16), "ctx", scatter_dimension=0, tiled=True
-            ).astype(jnp.float32)
+            projected = ctx_scatter(
+                partial.astype(jnp.bfloat16).reshape(ctx_size, span, partial.shape[1]), 0
+            )
             query = rotate(projected[:, :q_cols].reshape(span, q_count, HEAD_DIM), positions)
             kv = projected[:, q_cols:].reshape(span, kv_count, 2, HEAD_DIM)
             kv = jnp.stack([rotate(kv[:, :, 0], positions), kv[:, :, 1]], axis=2)
-            kv = lax.all_gather(
-                kv.astype(jnp.bfloat16).reshape(span, kv_count * 2 * HEAD_DIM),
-                "ctx",
-                axis=0,
-                tiled=True,
+            kv = ctx_gather(
+                kv.astype(jnp.bfloat16).reshape(span, kv_count * 2 * HEAD_DIM), 1
             ).reshape(ctx_size * span, kv_count, 2, HEAD_DIM)
             attended = attend(query.astype(jnp.bfloat16), kv[:, :, 0], kv[:, :, 1], positions)
-            attended = lax.all_gather(attended, "ctx", axis=0, tiled=True)
+            attended = ctx_gather(attended, 2)
             partial = jnp.dot(attended, combine[layer], preferred_element_type=jnp.float32)
             partial = partial.astype(jnp.bfloat16).reshape(ctx_size, span, slab)
             summed = lax.psum_scatter(
@@ -209,7 +500,7 @@
 def per_device(tokens, norm_gain, query_weight, keyval_weight, output_weight):
     layers = lax.axis_size("pipe")
     kv_count = keyval_weight.shape[2] // (2 * HEAD_DIM)
-    even = kv_count % layers == 0 and tokens.shape[1] % (16 * layers) == 0
+    even = lax.axis_size("ctx") % 2 == 0 and kv_count % layers == 0 and tokens.shape[1] % (16 * layers) == 0
     step = spread if even else gathered
     return step(tokens, norm_gain, query_weight, keyval_weight, output_weight)
 

time: 527 us -> 402 us (0.76)
  waiting for transfers between devices: 394 us -> 80.2 us
  Pallas kernels: 0 us -> 178 us
  local copies, waits for them, and re-layouts: 22.4 us -> 40.2 us
  blocking collectives: 40.8 us -> 34.5 us
    pallas_call x0 -> x6, Pallas kernels: none -> 178 us  [the longest x4 89.7 us: ctx_gather(): pl.pallas_call(functools.partial(gather_kernel, rows // 2), out_shape=jax...]
    all_gather x4 -> x0, waiting for transfers between devices: 166 us -> none  [the longest x2 92.6 us: spread(): attended = lax.all_gather(attended, 'ctx', axis=0, tiled=True)]
    reduce_scatter x2 -> x0, waiting for transfers between devices: 148 us -> none  [spread(): lax.psum_scatter(partial.astype(jnp.bfloat16), 'ctx', scatter_dimension=0...]
    unnamed x28, local copies, waits for them, and re-layouts: 8.07 us -> 16.6 us
    all_to_all x1 -> x0, blocking collectives: 6.3 us -> none  [swap_halves(): return lax.all_to_all(blocks, 'pipe', 0, 0)]
    all_to_all x2 -> x3, starting transfers between devices: 8.24 us -> 13 us  [swap_halves(): return lax.all_to_all(blocks, 'pipe', 0, 0)]
  transfers between devices with their start and end apart: 14 -> 9, of which waited for: 12 -> 6; matrix products, arithmetic and copies ran while one was open for 3% -> 8% of each run, Pallas kernels for 0% -> 22%
where the time goes in v2:
time: 402 us; the launch traced here: 401 us
  Pallas kernels  178 us (44%)
  waiting for transfers between devices  80.2 us (20%)
  local copies, waits for them, and re-layouts  40.2 us (10%)
  blocking collectives  34.5 us (9%)
  starting transfers between devices  24.2 us (6%)
  matrix products  22.6 us (6%)
  between operations  13.7 us (3%)
  other arithmetic  7.91 us (2%)
    pallas_call x4, Pallas kernels, ctx_gather(): pl.pallas_call(functools.partial(gather_kernel, rows // 2), out_shape=jax...  89.7 us
    pallas_call x2, Pallas kernels, ctx_scatter(): pl.pallas_call(functools.partial(scatter_kernel, cut), out_shape=jax.Shap...  87.8 us
    reduce_scatter x2, waiting for transfers between devices, spread(): lax.psum_scatter(partial, ('tp', 'pipe'), scatter_dimension=1, tiled=True)  47.1 us
    all_to_all x2, blocking collectives, spread(): sliced = lax.all_to_all(normed.reshape(mine, ctx_size, slab), 'ctx', 1, 0)  28.1 us
    all_to_all x2, waiting for transfers between devices, spread(): summed = lax.all_to_all(summed, 'ctx', 0, 1)  17.4 us
    unnamed x28, local copies, waits for them, and re-layouts  16.6 us
    all_gather x2, waiting for transfers between devices, spread(): everyone = lax.all_gather(sliced, ('tp', 'pipe'), axis=1, tiled=True)  14.9 us
    all_to_all x3, starting transfers between devices, swap_halves(): return lax.all_to_all(blocks, 'pipe', 0, 0)  13 us
  transfers between devices with their start and end apart: 9, of which 6 were waited for; matrix products, arithmetic and copies ran while one was open for 8% of the time, Pallas kernels for 22%

profile of v2, /device:TPU:0, one launch (start us, length us, event | category | flops | bytes accessed | tf_op | source)
XLA Modules:
  0.0 400.7 jit_solution(17768959182324330171)
XLA Ops:
  6.5 1.3 fusion.37
  7.8 1.0 dynamic-slice_convert_fusion
  8.8 2.2 all-gather.2
  11.6 16.2 %all_to_all.68 = bf16[1,32,8,512]{3,1,0,2:T(8,128)(2,1)S(1)} all-to-all(bf16[1,32,8,512]{3,1,0,2:T(8,128)(2,1)S(1)} %copy.82), channel_id=1, replica_groups=mesh['pipe'=2,'ctx'=8,'tp'=2] {'ctx'}, dimensions={2} | all-to-all | bytes 524288 | tf_op jit(solution)/shard_map/all_to_all | solution.py:471
  28.7 2.5 copy.85
  31.2 3.8 all-to-all-start.1
  35.0 2.3 constant_dynamic-slice_fusion
  37.3 2.3 copy.114
  39.6 4.4 %all-to-all-start.2 = ((bf16[2,512,512]{1,2,0:T(8,128)(2,1)}), bf16[2,512,512]{1,2,0:T(8,128)(2,1)}, u32[]{:S(2)}, u32[]{:S(2)}) async-start(bf16[2,512,512]{1,2,0:T(8,128)(2,1)} %bitcast.174), calls=%async_computation.2 | async-start | bytes 2097152 | tf_op jit(solution)/shard_map/all_to_all | solution.py:420
  44.1 1.5 constant_dynamic-update-slice_fusion.1
  46.3 4.8 %all-to-all-start.3 = ((bf16[2,1024,512]{2,1,0:T(8,128)(2,1)}), bf16[2,1024,512]{2,1,0:T(8,128)(2,1)}, u32[]{:S(2)}, u32[]{:S(2)}) async-start(bf16[2,1024,512]{2,1,0:T(8,128)(2,1)} %bitcast.179), calls=%async_computation.3 | async-start | bytes 4194304 | tf_op jit(solution)/shard_map/all_to_all | solution.py:420
  51.2 2.3 constant_dynamic-update-slice_fusion
  53.9 1.5 copy.84
  55.5 4.9 %convolution_convert_fusion.1 = bf16[1024,1536]{1,0:T(8,128)(2,1)} fusion(bf16[1024,512]{1,0:T(8,128)(2,1)S(1)} %bitcast.193, bf16[2,512,1536]{1,2,0:T(8,128)(2,1)} %constant_dynamic-update-slice_fusion), kind=kOutput, calls=%fused_computation.5 | convolution fusion | flops 1612185600 | bytes 5767168 | tf_op jit(solution)/shard_map/dot_general | solution.py:475
  60.4 44.2 %shard_map.55 = f32[128,1536]{1,0:T(8,128)} custom-call(bf16[8,128,1536]{2,1,0:T(8,128)(2,1)} %bitcast.176), custom_call_target="tpu_custom_call" | custom-call | tf_op jit(solution)/shard_map/pallas_call | solution.py:393
  106.0 1.1 slice_bitcast_fusion.9
  108.7 18.0 %shard_map.56 = bf16[8,128,512]{2,1,0:T(8,128)(2,1)} custom-call(bf16[128,512]{1,0:T(8,128)(2,1)} %convert_element_type.203.in_ref), custom_call_target="tpu_custom_call" | custom-call | tf_op jit(solution)/shard_map/pallas_call | solution.py:224
  126.7 1.3 reshape_reshape.6
  128.1 2.3 fusion.53
  130.8 2.3 copy.116
  133.1 1.0 fusion
  134.1 1.1 fusion.2
  135.3 1.2 fusion.27
  137.4 26.7 %shard_map.57 = bf16[8,128,1024]{2,1,0:T(8,128)(2,1)} custom-call(bf16[128,1024]{1,0:T(8,128)(2,1)} %copy.112.in_ref), custom_call_target="tpu_custom_call" | custom-call | tf_op jit(solution)/shard_map/pallas_call | solution.py:224
  164.0 4.2 %convolution_convert_fusion.3 = bf16[1024,512]{1,0:T(8,128)(2,1)} fusion(bf16[1024,1024]{1,0:T(8,128)(2,1)} %bitcast.177, bf16[2,1024,512]{2,1,0:T(8,128)(2,1)} %all-to-all-done.3), kind=kOutput, calls=%fused_computation.19 | convolution fusion | flops 1074266112 | bytes 4194304 | tf_op jit(solution)/shard_map/dot_general | solution.py:487
  168.2 24.0 %reduce-scatter.3.cloned.1.call-done = bf16[8,32,512]{2,1,0:T(8,128)(2,1)} async-done(((bf16[8,128,512]{2,1,0:T(8,128)(2,1)}), bf16[8,32,512]{2,1,0:T(8,128)(2,1)}) %reduce-scatter.3.cloned.1.call-update) | async-done | bytes 262160 | tf_op jit(solution)/shard_map/reduce_scatter | solution.py:489
  192.2 5.5 %all-to-all-start.4 = ((bf16[8,32,1,512]{3,1,2,0:T(8,128)(2,1)}), bf16[8,32,1,512]{3,1,2,0:T(8,128)(2,1)S(1)}, u32[]{:S(2)}, u32[]{:S(2)}) async-start(bf16[8,32,1,512]{3,1,2,0:T(8,128)(2,1)} %bitcast.196), calls=%async_computation.5 | async-start | bytes 524288 | tf_op jit(solution)/shard_map/all_to_all | solution.py:492
  197.8 8.7 %all-to-all-done.4 = bf16[8,32,1,512]{3,1,2,0:T(8,128)(2,1)S(1)} async-done(((bf16[8,32,1,512]{3,1,2,0:T(8,128)(2,1)}), bf16[8,32,1,512]{3,1,2,0:T(8,128)(2,1)S(1)}, u32[]{:S(2)}, u32[]{:S(2)}) %all-to-all-start.4) | async-done | bytes 262176 | tf_op jit(solution)/shard_map/all_to_all | solution.py:492
  207.5 12.0 %all_to_all.69 = bf16[1,32,8,512]{3,1,0,2:T(8,128)(2,1)S(1)} all-to-all(bf16[1,32,8,512]{3,1,0,2:T(8,128)(2,1)S(1)} %copy.97), channel_id=1, replica_groups=mesh['pipe'=2,'ctx'=8,'tp'=2] {'ctx'}, dimensions={2} | all-to-all | bytes 524288 | tf_op jit(solution)/shard_map/all_to_all | solution.py:471
  220.4 14.9 %all-gather.8.cloned.1.call-done = bf16[8,1,128,1,512]{4,0,3,1,2:T(8,128)(2,1)} async-done(((bf16[8,1,32,1,512]{4,0,3,1,2:T(8,128)(2,1)}), bf16[8,1,128,1,512]{4,0,3,1,2:T(8,128)(2,1)}) %all-gather.8.cloned.1.call-update) | async-done | bytes 1048592 | tf_op jit(solution)/shard_map/all_gather | solution.py:473
  235.2 1.5 copy.99
  236.8 4.9 %convolution_convert_fusion = bf16[1024,1536]{1,0:T(8,128)(2,1)} fusion(bf16[1024,512]{1,0:T(8,128)(2,1)S(1)} %bitcast.192, bf16[2,512,1536]{1,2,0:T(8,128)(2,1)} %constant_dynamic-update-slice_fusion), kind=kOutput, calls=%fused_computation.4 | convolution fusion | flops 1612185600 | bytes 5767168 | tf_op jit(solution)/shard_map/dot_general | solution.py:475
  241.7 43.7 %shard_map.58 = f32[128,1536]{1,0:T(8,128)} custom-call(bf16[8,128,1536]{2,1,0:T(8,128)(2,1)} %bitcast.175), custom_call_target="tpu_custom_call" | custom-call | tf_op jit(solution)/shard_map/pallas_call | solution.py:393
  286.8 1.9 slice_bitcast_fusion.8
  290.3 18.6 %shard_map.59 = bf16[8,128,512]{2,1,0:T(8,128)(2,1)} custom-call(bf16[128,512]{1,0:T(8,128)(2,1)} %convert_element_type.223.in_ref), custom_call_target="tpu_custom_call" | custom-call | tf_op jit(solution)/shard_map/pallas_call | solution.py:224
  308.8 1.3 reshape_reshape.7
  310.2 2.3 fusion.52
  312.5 1.2 copy.124
  314.1 2.3 copy.118
  316.3 1.0 fusion.1
  317.4 1.1 fusion.4
  318.5 1.2 fusion.21
  320.6 26.5 %shard_map.60 = bf16[8,128,1024]{2,1,0:T(8,128)(2,1)} custom-call(bf16[128,1024]{1,0:T(8,128)(2,1)} %copy.113.in_ref), custom_call_target="tpu_custom_call" | custom-call | tf_op jit(solution)/shard_map/pallas_call | solution.py:224
  347.1 4.1 %convolution_convert_fusion.2 = bf16[1024,512]{1,0:T(8,128)(2,1)} fusion(bf16[1024,1024]{1,0:T(8,128)(2,1)} %bitcast.178, bf16[2,1024,512]{2,1,0:T(8,128)(2,1)} %all-to-all-done.3), kind=kOutput, calls=%fused_computation.18 | convolution fusion | flops 1074266112 | bytes 4194304 | tf_op jit(solution)/shard_map/dot_general | solution.py:487
  351.2 23.1 %reduce-scatter.5.cloned.1.call-done = bf16[8,32,512]{2,1,0:T(8,128)(2,1)} async-done(((bf16[8,128,512]{2,1,0:T(8,128)(2,1)}), bf16[8,32,512]{2,1,0:T(8,128)(2,1)}) %reduce-scatter.5.cloned.1.call-update) | async-done | bytes 262160 | tf_op jit(solution)/shard_map/reduce_scatter | solution.py:489
  374.3 5.5 %all-to-all-start.6 = ((bf16[8,32,1,512]{3,1,2,0:T(8,128)(2,1)}), bf16[8,32,1,512]{3,1,2,0:T(8,128)(2,1)S(1)}, u32[]{:S(2)}, u32[]{:S(2)}) async-start(bf16[8,32,1,512]{3,1,2,0:T(8,128)(2,1)} %bitcast.197), calls=%async_computation.8 | async-start | bytes 524288 | tf_op jit(solution)/shard_map/all_to_all | solution.py:492
  380.0 8.7 %all-to-all-done.6 = bf16[8,32,1,512]{3,1,2,0:T(8,128)(2,1)S(1)} async-done(((bf16[8,32,1,512]{3,1,2,0:T(8,128)(2,1)}), bf16[8,32,1,512]{3,1,2,0:T(8,128)(2,1)S(1)}, u32[]{:S(2)}, u32[]{:S(2)}) %all-to-all-start.6) | async-done | bytes 262176 | tf_op jit(solution)/shard_map/all_to_all | solution.py:492
  389.3 4.2 %all_to_all.70 = bf16[2,32,4096]{2,1,0:T(8,128)(2,1)S(1)} all-to-all(bf16[2,32,4096]{2,1,0:T(8,128)(2,1)S(1)} %pad_maximum_fusion), channel_id=1, replica_groups=mesh['pipe'=2,'ctx'=8,'tp'=2] {'pipe'}, dimensions={0} | all-to-all | bytes 1048576 | tf_op jit(solution)/shard_map/all_to_all | solution.py:496
  (81 shorter events, 14.6 us)
Async XLA Ops:
  6.5 22.1 %copy-start.2 = (bf16[1,512,2048]{2,1,0:T(8,128)(2,1)S(1)}, bf16[1,512,2048]{2,1,0:T(8,128)(2,1)}, u32[]{:S(2)}) copy-start(bf16[1,512,2048]{2,1,0:T(8,128)(2,1)} %param.7) | copy-start | bytes 6291460
  6.5 47.4 %all-gather.6.cloned.1.call-start = ((), (), s32[]{:S(2)}) async-start(), calls=%async_computation.12 | async-start | bytes 1310720 | tf_op jit(solution)/shard_map/all_gather | solution.py:473
  31.2 8.4 %all-to-all-start.1 = ((bf16[2,512,1024]{1,2,0:T(8,128)(2,1)}), bf16[2,512,1024]{1,2,0:T(8,128)(2,1)S(1)}, u32[]{:S(2)}, u32[]{:S(2)}) async-start(bf16[2,512,1024]{1,2,0:T(8,128)(2,1)} %bitcast.169), calls=%async_computation.1 | async-start | bytes 4194304 | tf_op jit(solution)/shard_map/all_to_all | solution.py:420
  39.6 6.7 %all-to-all-start.2 = ((bf16[2,512,512]{1,2,0:T(8,128)(2,1)}), bf16[2,512,512]{1,2,0:T(8,128)(2,1)}, u32[]{:S(2)}, u32[]{:S(2)}) async-start(bf16[2,512,512]{1,2,0:T(8,128)(2,1)} %bitcast.174), calls=%async_computation.2 | async-start | bytes 2097152 | tf_op jit(solution)/shard_map/all_to_all | solution.py:420
  46.3 117.7 %all-to-all-start.3 = ((bf16[2,1024,512]{2,1,0:T(8,128)(2,1)}), bf16[2,1024,512]{2,1,0:T(8,128)(2,1)}, u32[]{:S(2)}, u32[]{:S(2)}) async-start(bf16[2,1024,512]{2,1,0:T(8,128)(2,1)} %bitcast.179), calls=%async_computation.3 | async-start | bytes 4194304 | tf_op jit(solution)/shard_map/all_to_all | solution.py:420
  51.1 141.1 %reduce-scatter.3.cloned.1.call-start = ((), (), s32[]{:S(2)}) async-start(), calls=%async_computation.10 | async-start | bytes 1310720 | tf_op jit(solution)/shard_map/reduce_scatter | solution.py:489
  130.4 2.8 copy-start.1
  133.1 2.2 copy-start.6
  164.0 43.0 %copy-start.3 = (bf16[1,64,4096]{2,1,0:T(8,128)(2,1)S(1)}, bf16[1,64,4096]{2,1,0:T(8,128)(2,1)}, u32[]{:S(2)}) copy-start(bf16[1,64,4096]{2,1,0:T(8,128)(2,1)} %param.5) | copy-start | bytes 1572868
  192.2 14.3 %all-to-all-start.4 = ((bf16[8,32,1,512]{3,1,2,0:T(8,128)(2,1)}), bf16[8,32,1,512]{3,1,2,0:T(8,128)(2,1)S(1)}, u32[]{:S(2)}, u32[]{:S(2)}) async-start(bf16[8,32,1,512]{3,1,2,0:T(8,128)(2,1)} %bitcast.196), calls=%async_computation.5 | async-start | bytes 524288 | tf_op jit(solution)/shard_map/all_to_all | solution.py:492
  197.7 37.5 %all-gather.8.cloned.1.call-start = ((), (), s32[]{:S(2)}) async-start(), calls=%async_computation.13 | async-start | bytes 1310720 | tf_op jit(solution)/shard_map/all_gather | solution.py:473
  220.3 154.0 %reduce-scatter.5.cloned.1.call-start = ((), (), s32[]{:S(2)}) async-start(), calls=%async_computation.11 | async-start | bytes 1310720 | tf_op jit(solution)/shard_map/reduce_scatter | solution.py:489
  312.5 3.9 copy-start
  316.3 2.2 copy-start.5
  351.2 37.9 %copy-start.4 = (bf16[1,64,4096]{2,1,0:T(8,128)(2,1)S(1)}, bf16[1,64,4096]{2,1,0:T(8,128)(2,1)}, u32[]{:S(2)}) copy-start(bf16[1,64,4096]{2,1,0:T(8,128)(2,1)} %param.5) | copy-start | bytes 1572868
  374.3 14.3 %all-to-all-start.6 = ((bf16[8,32,1,512]{3,1,2,0:T(8,128)(2,1)}), bf16[8,32,1,512]{3,1,2,0:T(8,128)(2,1)S(1)}, u32[]{:S(2)}, u32[]{:S(2)}) async-start(bf16[8,32,1,512]{3,1,2,0:T(8,128)(2,1)} %bitcast.197), calls=%async_computation.8 | async-start | bytes 524288 | tf_op jit(solution)/shard_map/all_to_all | solution.py:492
Sparse Core Ops, SparseCore 0:
  28.8 15.7 all-gather.5
  168.4 23.7 reduce-scatter.2
  220.4 14.7 all-gather.7
  351.4 22.9 reduce-scatter.4
